TPU v7x, 32 devices: a whole 2x2x4 slice. The times are simulated.
32 devices in a mesh: row: 4 (over y, x), col: 8 (over z, core).
Axes of the slice: x: 2, y: 2, z: 4, core: 2. Of those that a mesh axis runs over, the one named last changes fastest.
Arguments:
- hist_corr: float32 [16384, 16384], P('row', 'col'), may hold values from -1 to 1
- hist_resp: float32 [16384, 16384], P('row', 'col'), may hold values from -1 to 1, as said below
- row_corr: float32 [128, 16384], P(None, 'col'), may hold values from -1 to 1
- row_resp: float32 [128, 16384], P(None, 'col'), may hold values from -1 to 1
Outputs:
- final_corr: float32 [128, 16384], P(None, 'col')
- final_resp: float32 [128, 16384], P(None, 'col')
Inputs may be any that keep to these rules, and one draw needn't show every extreme that they name: hist_resp[s, u] is 0 where u > s and 1 where u == s.
All inputs are finite; a program needn't handle non-finite values.
Results may differ from a plain program's by a relative error of at most 0.00015.
Values sent between devices are 32-bit elements; how exact they have to be, the bound alone decides.
A program may use at most 128 MiB of HBM per device.

v0:
```python
import math

import jax
import jax.numpy as jnp
from jax import lax
from jax.sharding import PartitionSpec as P

HIST = 16384
BLOCKS = 4


step_size = 0.2
heat_reservoir_warmth = 0.6


def turn_rows(values):
    row_count = lax.axis_size("row")
    col_count = lax.axis_size("col")
    my_row = lax.axis_index("row")
    piece_span = values.shape[1] // row_count
    piece = lax.dynamic_slice_in_dim(values, my_row * piece_span, piece_span, 1)
    spread = jnp.broadcast_to(piece[None, None], (col_count, 1) + piece.shape)
    moved = lax.all_to_all(
        lax.all_to_all(spread, "col", split_axis=0, concat_axis=1, tiled=True),
        "row",
        split_axis=1,
        concat_axis=0,
        tiled=True,
    )
    return jnp.transpose(moved, (2, 1, 0, 3)).reshape(piece.shape[0], -1)


def turn_cols(values):
    row_count = lax.axis_size("row")
    col_count = lax.axis_size("col")
    my_col = lax.axis_index("col")
    factor = col_count // row_count
    block_span = values.shape[1] // factor
    piece_span = block_span // col_count
    blocks = values.reshape(values.shape[0], factor, block_span)
    piece = lax.dynamic_slice_in_dim(blocks, my_col * piece_span, piece_span, 2)
    ordered = jnp.transpose(piece, (1, 0, 2))
    spread = jnp.broadcast_to(ordered[None], (row_count,) + ordered.shape)
    moved = lax.all_to_all(
        lax.all_to_all(spread, "row", split_axis=0, concat_axis=1, tiled=True),
        "col",
        split_axis=1,
        concat_axis=0,
        tiled=True,
    )
    return jnp.transpose(moved[:, 0], (1, 0, 2)).reshape(values.shape[0], -1)


def energy_layout(values):
    return turn_rows(values)


def cross_layout(values):
    return turn_cols(values)


def advance(
    autocovariance_curve,
    perturbation_reaction,
    memory_corr,
    memory_resp,
    cross_term,
    norm_enforcing_scalar,
    integration_coefficient,
):
    next_corr = autocovariance_curve + step_size * (
        integration_coefficient * (memory_corr + cross_term)
        - norm_enforcing_scalar * autocovariance_curve
    )
    next_resp = perturbation_reaction + step_size * (
        integration_coefficient * memory_resp - norm_enforcing_scalar * perturbation_reaction
    )
    return (next_corr, next_resp)


def body(hist_corr, hist_resp, row_corr, row_resp):
    highest = lax.Precision.HIGHEST
    integration_coefficient = 1.0 / math.sqrt(HIST)
    autocovariance_curve = row_corr
    perturbation_reaction = row_resp
    for block_index in range(BLOCKS):
        history_integrand = 3.0 * autocovariance_curve * perturbation_reaction
        slope_contribution = 1.5 * autocovariance_curve * autocovariance_curve
        multiplier_terms = jnp.sum(
            history_integrand * autocovariance_curve + slope_contribution * perturbation_reaction,
            axis=1,
        )
        part_cross = lax.dot_general(
            slope_contribution,
            hist_resp,
            (((1,), (1,)), ((), ())),
            precision=highest,
            preferred_element_type=jnp.float32,
        )
        enforcing_scalar_sum = lax.psum(multiplier_terms, "col")
        energy_rows = energy_layout(history_integrand)
        cross_total = lax.psum(part_cross, "col")
        cross_term = cross_layout(cross_total)
        norm_enforcing_scalar = (
            heat_reservoir_warmth + integration_coefficient * enforcing_scalar_sum[:, None]
        )
        part_corr = jnp.dot(
            energy_rows, hist_corr, precision=highest, preferred_element_type=jnp.float32
        )
        part_resp = jnp.dot(
            energy_rows, hist_resp, precision=highest, preferred_element_type=jnp.float32
        )
        memory_corr, memory_resp = lax.psum((part_corr, part_resp), "row")
        autocovariance_curve, perturbation_reaction = advance(
            autocovariance_curve,
            perturbation_reaction,
            memory_corr,
            memory_resp,
            cross_term,
            norm_enforcing_scalar,
            integration_coefficient,
        )
    return (autocovariance_curve, perturbation_reaction)


def solution(mesh):
    in_specs = (P("row", "col"), P("row", "col"), P(None, "col"), P(None, "col"))
    out_specs = (P(None, "col"), P(None, "col"))
    return jax.shard_map(body, mesh=mesh, in_specs=in_specs, out_specs=out_specs, check_vma=False)
```

profile of v0, /device:TPU:0, one launch (start us, length us, event | category | flops | bytes accessed | tf_op | source)
XLA Modules:
  0.0 1180.6 jit_solution(5139241333706496647)
XLA Ops:
  10.2 55.3 %all_to_all.180 = f32[8,1,128,512]{3,2,1,0:T(8,128)} all-to-all(f32[8,1,128,512]{3,2,1,0:T(8,128)S(1)} %broadcast_in_dim.16), channel_id=1, replica_groups=mesh['row'=4,'col'=8] {'col'}, dimensions={0} | all-to-all | bytes 4194304 | tf_op jit(solution)/shard_map/all_to_all | solution.py:24
  65.5 4.6 all-to-all-start.1
  70.1 37.2 %fusion = f32[128,4096]{1,0:T(8,128)S(1)} fusion(f32[4096,2048]{1,0:T(8,128)} %param.5, f32[128,2048]{1,0:T(8,128)S(1)} %copy-done.4), kind=kOutput, calls=%fused_computation.20 | convolution fusion | flops 12885426176 | bytes 36700160 | tf_op jit(solution)/shard_map/dot_general | solution.py:93
  110.3 64.6 %all-reduce.13.cloned.1.call-done = f32[128,2,2048]{2,1,0:T(2,128)} async-done(((f32[128,2,2048]{2,1,0:T(2,128)}), f32[128,2,2048]{2,1,0:T(2,128)}) %all-reduce.13.cloned.1.call-update) | async-done | bytes 2097168 | tf_op jit(solution)/shard_map/psum | solution.py:102
  183.8 22.4 %fusion.13 = f32[128,2048]{1,0:T(8,128)} fusion(f32[128,4096]{0,1:T(8,128)S(1)} %bitcast.88, f32[4096,2048]{1,0:T(8,128)} %param.5), kind=kOutput, calls=%fused_computation.45 | convolution fusion | flops 12884901888 | bytes 36700160 | tf_op jit(solution)/shard_map/dot_general | solution.py:110
  206.2 22.4 %fusion.12 = f32[128,2048]{1,0:T(8,128)} fusion(f32[128,4096]{0,1:T(8,128)S(1)} %bitcast.89, f32[4096,2048]{1,0:T(8,128)} %param.4), kind=kOutput, calls=%fused_computation.44 | convolution fusion | flops 12884901888 | bytes 36700160 | tf_op jit(solution)/shard_map/dot_general | solution.py:107
  234.6 29.3 %psum.114 = f32[128]{0:T(128)S(1)} all-reduce(f32[128]{0:T(128)S(1)} %get-tuple-element.20), channel_id=1, replica_groups=mesh['row'=4,'col'=8] {'col'}, use_global_device_ids=true, to_apply=%region_3.0 | all-reduce | flops 128 | bytes 1024 | tf_op jit(solution)/shard_map/psum | solution.py:100
  265.0 33.0 %all-reduce.27.cloned.1.call-done = (f32[128,2048]{1,0:T(8,128)}, f32[128,2048]{1,0:T(8,128)}) async-done(((f32[128,2048]{1,0:T(8,128)}, f32[128,2048]{1,0:T(8,128)}), (f32[128,2048]{1,0:T(8,128)}, f32[128,2048]{1,0:T(8,128)})) %all-reduce.27.cloned.1.call-update) | async-done | bytes 2097168 | tf_op jit(solution)/shard_map/psum | solution.py:113
  301.4 53.5 %all_to_all.181 = f32[8,1,128,512]{3,2,1,0:T(8,128)} all-to-all(f32[8,1,128,512]{3,2,1,0:T(8,128)S(1)} %broadcast_in_dim.18), channel_id=1, replica_groups=mesh['row'=4,'col'=8] {'col'}, dimensions={0} | all-to-all | bytes 4194304 | tf_op jit(solution)/shard_map/all_to_all | solution.py:24
  355.0 4.5 all-to-all-start.5
  359.7 39.0 %fusion.1 = f32[128,4096]{1,0:T(8,128)} fusion(f32[4096,2048]{1,0:T(8,128)} %param.5, f32[128,2048]{1,0:T(8,128)S(1)} %get-tuple-element.18), kind=kOutput, calls=%fused_computation.21 | convolution fusion | flops 12885426176 | bytes 36700160 | tf_op jit(solution)/shard_map/dot_general | solution.py:93
  402.7 64.6 %all-reduce.15.cloned.1.call-done = f32[128,2,2048]{2,1,0:T(2,128)} async-done(((f32[128,2,2048]{2,1,0:T(2,128)}), f32[128,2,2048]{2,1,0:T(2,128)}) %all-reduce.15.cloned.1.call-update) | async-done | bytes 2097168 | tf_op jit(solution)/shard_map/psum | solution.py:102
  476.0 22.4 %fusion.15 = f32[128,2048]{1,0:T(8,128)} fusion(f32[128,4096]{0,1:T(8,128)S(1)} %bitcast.90, f32[4096,2048]{1,0:T(8,128)} %param.5), kind=kOutput, calls=%fused_computation.47 | convolution fusion | flops 12884901888 | bytes 36700160 | tf_op jit(solution)/shard_map/dot_general | solution.py:110
  498.4 22.4 %fusion.14 = f32[128,2048]{1,0:T(8,128)} fusion(f32[128,4096]{0,1:T(8,128)S(1)} %bitcast.91, f32[4096,2048]{1,0:T(8,128)} %param.4), kind=kOutput, calls=%fused_computation.46 | convolution fusion | flops 12884901888 | bytes 36700160 | tf_op jit(solution)/shard_map/dot_general | solution.py:107
  526.9 29.3 %psum.118 = f32[128]{0:T(128)S(1)} all-reduce(f32[128]{0:T(128)S(1)} %get-tuple-element.16), channel_id=1, replica_groups=mesh['row'=4,'col'=8] {'col'}, use_global_device_ids=true, to_apply=%region_8.0 | all-reduce | flops 128 | bytes 1024 | tf_op jit(solution)/shard_map/psum | solution.py:100
  557.3 32.9 %all-reduce.25.cloned.1.call-done = (f32[128,2048]{1,0:T(8,128)}, f32[128,2048]{1,0:T(8,128)}) async-done(((f32[128,2048]{1,0:T(8,128)}, f32[128,2048]{1,0:T(8,128)}), (f32[128,2048]{1,0:T(8,128)}, f32[128,2048]{1,0:T(8,128)})) %all-reduce.25.cloned.1.call-update) | async-done | bytes 2097168 | tf_op jit(solution)/shard_map/psum | solution.py:113
  593.9 53.5 %all_to_all.182 = f32[8,1,128,512]{3,2,1,0:T(8,128)} all-to-all(f32[8,1,128,512]{3,2,1,0:T(8,128)S(1)} %broadcast_in_dim.20), channel_id=1, replica_groups=mesh['row'=4,'col'=8] {'col'}, dimensions={0} | all-to-all | bytes 4194304 | tf_op jit(solution)/shard_map/all_to_all | solution.py:24
  647.4 4.5 all-to-all-start.9
  652.3 37.2 %fusion.2 = f32[128,4096]{1,0:T(8,128)S(1)} fusion(f32[4096,2048]{1,0:T(8,128)} %param.5, f32[128,2048]{1,0:T(8,128)S(1)} %get-tuple-element.15), kind=kOutput, calls=%fused_computation.22 | convolution fusion | flops 12885426176 | bytes 36700160 | tf_op jit(solution)/shard_map/dot_general | solution.py:93
  692.4 64.6 %all-reduce.17.cloned.1.call-done = f32[128,2,2048]{2,1,0:T(2,128)} async-done(((f32[128,2,2048]{2,1,0:T(2,128)}), f32[128,2,2048]{2,1,0:T(2,128)}) %all-reduce.17.cloned.1.call-update) | async-done | bytes 2097168 | tf_op jit(solution)/shard_map/psum | solution.py:102
  765.7 22.4 %fusion.17 = f32[128,2048]{1,0:T(8,128)} fusion(f32[128,4096]{0,1:T(8,128)S(1)} %bitcast.92, f32[4096,2048]{1,0:T(8,128)} %param.5), kind=kOutput, calls=%fused_computation.49 | convolution fusion | flops 12884901888 | bytes 36700160 | tf_op jit(solution)/shard_map/dot_general | solution.py:110
  788.2 22.4 %fusion.16 = f32[128,2048]{1,0:T(8,128)} fusion(f32[128,4096]{0,1:T(8,128)S(1)} %bitcast.93, f32[4096,2048]{1,0:T(8,128)} %param.4), kind=kOutput, calls=%fused_computation.48 | convolution fusion | flops 12884901888 | bytes 36700160 | tf_op jit(solution)/shard_map/dot_general | solution.py:107
  816.6 29.3 %psum.122 = f32[128]{0:T(128)S(1)} all-reduce(f32[128]{0:T(128)S(1)} %get-tuple-element.13), channel_id=1, replica_groups=mesh['row'=4,'col'=8] {'col'}, use_global_device_ids=true, to_apply=%region_13.0 | all-reduce | flops 128 | bytes 1024 | tf_op jit(solution)/shard_map/psum | solution.py:100
  847.1 32.9 %all-reduce.23.cloned.1.call-done = (f32[128,2048]{1,0:T(8,128)}, f32[128,2048]{1,0:T(8,128)}) async-done(((f32[128,2048]{1,0:T(8,128)}, f32[128,2048]{1,0:T(8,128)}), (f32[128,2048]{1,0:T(8,128)}, f32[128,2048]{1,0:T(8,128)})) %all-reduce.23.cloned.1.call-update) | async-done | bytes 2097168 | tf_op jit(solution)/shard_map/psum | solution.py:113
  883.6 53.5 %all_to_all.183 = f32[8,1,128,512]{3,2,1,0:T(8,128)} all-to-all(f32[8,1,128,512]{3,2,1,0:T(8,128)S(1)} %broadcast_in_dim.22), channel_id=1, replica_groups=mesh['row'=4,'col'=8] {'col'}, dimensions={0} | all-to-all | bytes 4194304 | tf_op jit(solution)/shard_map/all_to_all | solution.py:24
  937.1 4.5 all-to-all-start.13
  941.8 37.2 %fusion.3 = f32[128,4096]{1,0:T(8,128)S(1)} fusion(f32[4096,2048]{1,0:T(8,128)} %param.5, f32[128,2048]{1,0:T(8,128)S(1)} %get-tuple-element.12), kind=kOutput, calls=%fused_computation.23 | convolution fusion | flops 12885426176 | bytes 36700160 | tf_op jit(solution)/shard_map/dot_general | solution.py:93
  982.0 64.6 %all-reduce.19.cloned.1.call-done = f32[128,2,2048]{2,1,0:T(2,128)} async-done(((f32[128,2,2048]{2,1,0:T(2,128)}), f32[128,2,2048]{2,1,0:T(2,128)}) %all-reduce.19.cloned.1.call-update) | async-done | bytes 2097168 | tf_op jit(solution)/shard_map/psum | solution.py:102
  1054.7 22.4 %fusion.19 = f32[128,2048]{1,0:T(8,128)} fusion(f32[128,4096]{0,1:T(8,128)S(1)} %bitcast.94, f32[4096,2048]{1,0:T(8,128)} %param.5), kind=kOutput, calls=%fused_computation.51 | convolution fusion | flops 12884901888 | bytes 36700160 | tf_op jit(solution)/shard_map/dot_general | solution.py:110
  1077.1 22.4 %fusion.18 = f32[128,2048]{1,0:T(8,128)} fusion(f32[128,4096]{0,1:T(8,128)S(1)} %bitcast.95, f32[4096,2048]{1,0:T(8,128)} %param.4), kind=kOutput, calls=%fused_computation.50 | convolution fusion | flops 12884901888 | bytes 36700160 | tf_op jit(solution)/shard_map/dot_general | solution.py:107
  1104.4 29.3 %psum.126 = f32[128]{0:T(128)S(1)} all-reduce(f32[128]{0:T(128)S(1)} %get-tuple-element.10), channel_id=1, replica_groups=mesh['row'=4,'col'=8] {'col'}, use_global_device_ids=true, to_apply=%region_18.0 | all-reduce | flops 128 | bytes 1024 | tf_op jit(solution)/shard_map/psum | solution.py:100
  1134.8 34.2 %all-reduce.21.cloned.1.call-done = (f32[128,2048]{1,0:T(8,128)}, f32[128,2048]{1,0:T(8,128)}) async-done(((f32[128,2048]{1,0:T(8,128)}, f32[128,2048]{1,0:T(8,128)}), (f32[128,2048]{1,0:T(8,128)}, f32[128,2048]{1,0:T(8,128)})) %all-reduce.21.cloned.1.call-update) | async-done | bytes 2097168 | tf_op jit(solution)/shard_map/psum | solution.py:113
  (98 shorter events, 91.4 us)
Async XLA Ops:
  65.5 4.7 copy-start.4
  65.5 110.4 %all-to-all-start.1 = ((f32[1,8,128,512]{3,2,0,1:T(8,128)}), f32[1,8,128,512]{3,2,0,1:T(8,128)}, u32[]{:S(2)}, u32[]{:S(2)}) async-start(f32[1,8,128,512]{3,2,0,1:T(8,128)} %bitcast.1), calls=%async_computation.1 | async-start | bytes 4194304 | tf_op jit(solution)/shard_map/all_to_all | solution.py:23
  70.1 104.8 %all-reduce.13.cloned.1.call-start = ((), (), s32[]{:S(2)}) async-start(), calls=%async_computation.16 | async-start | bytes 4194304 | tf_op jit(solution)/shard_map/psum | solution.py:102
  177.1 51.6 %all-to-all-start.2 = ((f32[4,2,128,256]{3,1,2,0:T(2,128)}), f32[4,2,128,256]{3,1,2,0:T(2,128)}, u32[]{:S(2)}, u32[]{:S(2)}) async-start(f32[4,2,128,256]{3,1,2,0:T(2,128)} %broadcast_in_dim.17), calls=%async_computation.2 | async-start | bytes 2097152 | tf_op jit(solution)/shard_map/all_to_all | solution.py:45
  181.4 116.7 %all-reduce.27.cloned.1.call-start = ((), (), s32[]{:S(2)}) async-start(), calls=%async_computation.23 | async-start | bytes 4194304 | tf_op jit(solution)/shard_map/psum | solution.py:113
  231.0 32.9 %all-to-all-start.3 = ((f32[1,8,128,256]{3,2,0,1:T(8,128)}), f32[1,8,128,256]{3,2,0,1:T(8,128)S(1)}, u32[]{:S(2)}, u32[]{:S(2)}) async-start(f32[1,8,128,256]{3,2,0,1:T(8,128)} %bitcast.7), calls=%async_computation.3 | async-start | bytes 2097152 | tf_op jit(solution)/shard_map/all_to_all | solution.py:44
  301.0 58.7 %copy-start = (f32[128,2048]{1,0:T(8,128)}, f32[128,2048]{1,0:T(8,128)S(1)}, u32[]{:S(2)}) copy-start(f32[128,2048]{1,0:T(8,128)S(1)} %get-tuple-element.18) | copy-start | bytes 3145732
  355.0 113.3 %all-to-all-start.5 = ((f32[1,8,128,512]{3,2,0,1:T(8,128)}), f32[1,8,128,512]{3,2,0,1:T(8,128)}, u32[]{:S(2)}, u32[]{:S(2)}) async-start(f32[1,8,128,512]{3,2,0,1:T(8,128)} %bitcast.96), calls=%async_computation.5 | async-start | bytes 4194304 | tf_op jit(solution)/shard_map/all_to_all | solution.py:23
  359.5 107.9 %all-reduce.15.cloned.1.call-start = ((), (), s32[]{:S(2)}) async-start(), calls=%async_computation.17 | async-start | bytes 4194304 | tf_op jit(solution)/shard_map/psum | solution.py:102
  469.5 51.3 %all-to-all-start.6 = ((f32[4,2,128,256]{3,1,2,0:T(2,128)}), f32[4,2,128,256]{3,1,2,0:T(2,128)}, u32[]{:S(2)}, u32[]{:S(2)}) async-start(f32[4,2,128,256]{3,1,2,0:T(2,128)} %broadcast_in_dim.19), calls=%async_computation.6 | async-start | bytes 2097152 | tf_op jit(solution)/shard_map/all_to_all | solution.py:45
  473.8 116.4 %all-reduce.25.cloned.1.call-start = ((), (), s32[]{:S(2)}) async-start(), calls=%async_computation.22 | async-start | bytes 4194304 | tf_op jit(solution)/shard_map/psum | solution.py:113
  523.2 67.1 %copy-start.1 = (f32[128,2048]{1,0:T(8,128)S(1)}, f32[128,2048]{1,0:T(8,128)}, u32[]{:S(2)}) copy-start(f32[128,2048]{1,0:T(8,128)} %copy-done) | copy-start | bytes 3145732
  523.2 33.0 %all-to-all-start.7 = ((f32[1,8,128,256]{3,2,0,1:T(8,128)}), f32[1,8,128,256]{3,2,0,1:T(8,128)S(1)}, u32[]{:S(2)}, u32[]{:S(2)}) async-start(f32[1,8,128,256]{3,2,0,1:T(8,128)} %bitcast.101), calls=%async_computation.7 | async-start | bytes 2097152 | tf_op jit(solution)/shard_map/all_to_all | solution.py:44
  592.9 1.0 copy-start.5
  647.4 110.7 %all-to-all-start.9 = ((f32[1,8,128,512]{3,2,0,1:T(8,128)}), f32[1,8,128,512]{3,2,0,1:T(8,128)}, u32[]{:S(2)}, u32[]{:S(2)}) async-start(f32[1,8,128,512]{3,2,0,1:T(8,128)} %bitcast.21), calls=%async_computation.9 | async-start | bytes 4194304 | tf_op jit(solution)/shard_map/all_to_all | solution.py:23
  651.8 105.2 %all-reduce.17.cloned.1.call-start = ((), (), s32[]{:S(2)}) async-start(), calls=%async_computation.18 | async-start | bytes 4194304 | tf_op jit(solution)/shard_map/psum | solution.py:102
  759.3 51.3 %all-to-all-start.10 = ((f32[4,2,128,256]{3,1,2,0:T(2,128)}), f32[4,2,128,256]{3,1,2,0:T(2,128)}, u32[]{:S(2)}, u32[]{:S(2)}) async-start(f32[4,2,128,256]{3,1,2,0:T(2,128)} %broadcast_in_dim.21), calls=%async_computation.10 | async-start | bytes 2097152 | tf_op jit(solution)/shard_map/all_to_all | solution.py:45
  763.6 116.4 %all-reduce.23.cloned.1.call-start = ((), (), s32[]{:S(2)}) async-start(), calls=%async_computation.21 | async-start | bytes 4194304 | tf_op jit(solution)/shard_map/psum | solution.py:113
  812.9 67.0 %copy-start.6 = (f32[128,2048]{1,0:T(8,128)S(1)}, f32[128,2048]{1,0:T(8,128)}, u32[]{:S(2)}) copy-start(f32[128,2048]{1,0:T(8,128)} %copy-done.5) | copy-start | bytes 3145732
  812.9 33.0 %all-to-all-start.11 = ((f32[1,8,128,256]{3,2,0,1:T(8,128)}), f32[1,8,128,256]{3,2,0,1:T(8,128)S(1)}, u32[]{:S(2)}, u32[]{:S(2)}) async-start(f32[1,8,128,256]{3,2,0,1:T(8,128)} %bitcast.102), calls=%async_computation.11 | async-start | bytes 2097152 | tf_op jit(solution)/shard_map/all_to_all | solution.py:44
  882.6 1.0 copy-start.7
  882.6 59.2 %copy-start.2 = (f32[128,2048]{1,0:T(8,128)}, f32[128,2048]{1,0:T(8,128)S(1)}, u32[]{:S(2)}) copy-start(f32[128,2048]{1,0:T(8,128)S(1)} %get-tuple-element.12) | copy-start | bytes 3145732
  937.1 110.5 %all-to-all-start.13 = ((f32[1,8,128,512]{3,2,0,1:T(8,128)}), f32[1,8,128,512]{3,2,0,1:T(8,128)}, u32[]{:S(2)}, u32[]{:S(2)}) async-start(f32[1,8,128,512]{3,2,0,1:T(8,128)} %bitcast.31), calls=%async_computation.13 | async-start | bytes 4194304 | tf_op jit(solution)/shard_map/all_to_all | solution.py:23
  941.6 105.0 %all-reduce.19.cloned.1.call-start = ((), (), s32[]{:S(2)}) async-start(), calls=%async_computation.19 | async-start | bytes 4194304 | tf_op jit(solution)/shard_map/psum | solution.py:102
  1048.8 50.7 %all-to-all-start.14 = ((f32[4,2,128,256]{3,1,2,0:T(2,128)}), f32[4,2,128,256]{3,1,2,0:T(2,128)S(1)}, u32[]{:S(2)}, u32[]{:S(2)}) async-start(f32[4,2,128,256]{3,1,2,0:T(2,128)} %broadcast_in_dim.23), calls=%async_computation.14 | async-start | bytes 2097152 | tf_op jit(solution)/shard_map/all_to_all | solution.py:45
  1052.5 116.5 %all-reduce.21.cloned.1.call-start = ((), (), s32[]{:S(2)}) async-start(), calls=%async_computation.20 | async-start | bytes 4194304 | tf_op jit(solution)/shard_map/psum | solution.py:113
  1100.7 68.4 %copy-start.3 = (f32[128,2048]{1,0:T(8,128)S(1)}, f32[128,2048]{1,0:T(8,128)}, u32[]{:S(2)}) copy-start(f32[128,2048]{1,0:T(8,128)} %copy-done.2) | copy-start | bytes 3145732
  1100.7 68.4 %copy-start.8 = (f32[128,2048]{1,0:T(8,128)S(1)}, f32[128,2048]{1,0:T(8,128)}, u32[]{:S(2)}) copy-start(f32[128,2048]{1,0:T(8,128)} %copy-done.7) | copy-start | bytes 3145732
  1100.7 33.0 %all-to-all-start.15 = ((f32[1,8,128,256]{3,2,0,1:T(8,128)}), f32[1,8,128,256]{3,2,0,1:T(8,128)S(1)}, u32[]{:S(2)}, u32[]{:S(2)}) async-start(f32[1,8,128,256]{3,2,0,1:T(8,128)} %bitcast.103), calls=%async_computation.15 | async-start | bytes 2097152 | tf_op jit(solution)/shard_map/all_to_all | solution.py:44
Sparse Core Ops, SparseCore 0:
  110.4 64.4 all-reduce.12
  402.8 64.4 all-reduce.14
  692.6 64.4 all-reduce.16
  982.1 64.4 all-reduce.18
Sparse Core Ops, SparseCore 1:
  228.8 69.2 all-reduce.26
  521.0 69.2 all-reduce.24
  810.7 69.2 all-reduce.22
  1099.7 69.3 all-reduce.20
where the time goes:
time: 1190 us; the launch traced here: 1180 us
  waiting for transfers between devices  392 us (33%)
  blocking collectives  333 us (28%)
  matrix products  330 us (28%)
  starting transfers between devices  51.2 us (4%)
  local copies, waits for them, and re-layouts  43.7 us (4%)
  between operations  16.3 us (1%)
  other arithmetic  14.3 us (1%)
    psum x4, waiting for transfers between devices, body(): cross_total = lax.psum(part_cross, 'col')  258 us
    all_to_all x4, blocking collectives, turn_rows(): lax.all_to_all(spread, 'col', split_axis=0, concat_axis=1, tiled=True)  216 us
    dot_general x4, matrix products, body(): lax.dot_general(slope_contribution, hist_resp, (((1,), (1,)), ((), ())),...  151 us
    psum x4, waiting for transfers between devices, body(): memory_corr, memory_resp = lax.psum((part_corr, part_resp), 'row')  133 us
    psum x4, blocking collectives, body(): enforcing_scalar_sum = lax.psum(multiplier_terms, 'col')  117 us
    dot_general x4, matrix products, body(): jnp.dot(energy_rows, hist_resp, precision=highest, preferred_element_type...  89.7 us
    dot_general x4, matrix products, body(): jnp.dot(energy_rows, hist_corr, precision=highest, preferred_element_type...  89.7 us
  transfers between devices with their start and end apart: 20, of which 8 were waited for; matrix products, arithmetic and copies ran while one was open for 31% of the time, Pallas kernels for 0%

commit v1 on v0

v1 whole, which is shorter than its diff:
```python
import functools
import math

import jax
import jax.numpy as jnp
from jax import lax
from jax.experimental import pallas as pl
from jax.experimental.pallas import tpu as pltpu
from jax.sharding import PartitionSpec as P

BLOCKS = 4
STEP = 0.2
WARMTH = 0.6


def plain_body(hist_corr, hist_resp, row_corr, row_resp):
    rows = lax.axis_size("row")
    span = row_corr.shape[0] // rows
    coef = 1.0 / math.sqrt(hist_corr.shape[0] * rows)
    start = lax.axis_index("row") * span
    corr = lax.dynamic_slice_in_dim(row_corr, start, span, 0)
    resp = lax.dynamic_slice_in_dim(row_resp, start, span, 0)

    def dot(a, b, dims):
        return lax.dot_general(
            a, b, (dims, ((), ())), precision=lax.Precision.HIGH, preferred_element_type=jnp.float32
        )

    for _ in range(BLOCKS):
        energy = 3.0 * corr * resp
        slope = 1.5 * corr * corr
        mult = lax.psum(jnp.sum(energy * corr + slope * resp, axis=1), "col")
        full = lax.all_gather(corr, "row", axis=0, tiled=True)
        wide = lax.all_gather(energy, "col", axis=1, tiled=True)
        energy_rows = lax.all_to_all(wide, "row", split_axis=1, concat_axis=0, tiled=True)
        part_cross = dot(1.5 * full * full, hist_resp, ((1,), (1,)))
        turned = lax.all_to_all(part_cross, "row", split_axis=0, concat_axis=1, tiled=True)
        cross = lax.psum_scatter(turned, "col", scatter_dimension=1, tiled=True)
        part_corr = dot(energy_rows, hist_corr, ((1,), (0,)))
        part_resp = dot(energy_rows, hist_resp, ((1,), (0,)))
        mem_corr = lax.psum_scatter(part_corr, "row", scatter_dimension=0, tiled=True)
        mem_resp = lax.psum_scatter(part_resp, "row", scatter_dimension=0, tiled=True)
        scalar = WARMTH + coef * mult[:, None]
        next_corr = corr + STEP * (coef * (mem_corr + cross) - scalar * corr)
        resp = resp + STEP * (coef * mem_resp - scalar * resp)
        corr = next_corr
    return (
        lax.all_gather(corr, "row", axis=0, tiled=True),
        lax.all_gather(resp, "row", axis=0, tiled=True),
    )


MESH = pl.DeviceIdType.MESH
F32 = jnp.float32


SLOTS = 3
BF16 = jnp.bfloat16


def split(x):
    hi = x.astype(BF16)
    return hi, (x - hi.astype(F32)).astype(BF16)


def block_kernel(last, coef, R, Z, hc, hr, c_prev, c_in, r_in, *refs):
    refs = list(refs)
    take = lambda n: [refs.pop(0) for _ in range(n)]
    if last:
        c_full, r_full = take(2)
    else:
        c_out, r_out, c_full = take(3)
    tiles, xp, acc, e_rows, estack, dstack = take(6)
    xbuf, xsum, xin, up, mrecv, racc, csrc, eall, mbuf = take(9)
    (tsem,) = take(1)
    xs, xr, xis, xir, ups, upr, ms, mrs, cs, crs = take(10)
    eus, eur, eds, edr, eis, eir, ps, pr, mus, mur = take(10)
    assert not refs
    T, U = c_in.shape
    M = R * T
    N = 2 * Z
    CH = tiles.shape[1]
    per = U // CH
    count = 2 * per
    r, c = lax.axis_index("row"), lax.axis_index("col")
    z = lax.div(c, 2)
    k = c - 2 * z
    partner = 2 * z + 1 - k
    rows = [lax.rem(r + d, R) for d in range(1, R)]
    cols = [lax.rem(c + d, N) for d in range(1, N)]
    low = z <= r

    def rc(src, dst, ss, rs, row, col):
        return pltpu.make_async_remote_copy(
            src_ref=src, dst_ref=dst, send_sem=ss, recv_sem=rs, device_id=(row, col), device_id_type=MESH
        )

    def at_row(q):
        return pl.ds(pl.multiple_of(q * T, T), T)

    def half(h):
        return pl.ds(pl.multiple_of(h * U, U), U)

    def x_start(i):
        side = 1 - k if i < per else k
        return pl.multiple_of(side * U + (i % per) * CH, CH)

    def tile_copy(n):
        kind, i = divmod(n, count)
        start = x_start(i) if kind == 0 else i * CH
        src = hc if kind == 1 else hr
        return pltpu.make_async_copy(src.at[pl.ds(start, CH)], tiles.at[n % SLOTS], tsem.at[n % SLOTS])

    tile_copy(0).start()
    tile_copy(1).start()

    barrier = pltpu.get_barrier_semaphore()
    for q in rows:
        pl.semaphore_signal(barrier, inc=1, device_id=(q, c), device_id_type=MESH)
    for q in cols:
        pl.semaphore_signal(barrier, inc=1, device_id=(r, q), device_id_type=MESH)

    energy = 3.0 * c_in[...] * r_in[...]
    eall[z] = energy
    terms = energy * c_in[...] + 1.5 * c_in[...] * c_in[...] * r_in[...]
    part = terms[:, :128]
    for i in range(1, U // 128):
        part = part + terms[:, i * 128 : (i + 1) * 128]
    mbuf[c] = part
    pl.semaphore_wait(barrier, R - 1 + N - 1)

    def flow(p, step):
        ss, rs = (eus, eur) if step > 0 else (eds, edr)
        return rc(eall.at[p], eall.at[p], ss.at[p], rs.at[p], r, c + step)

    def inplane(d, p):
        return rc(eall.at[p], e_rows.at[at_row(r), half(k)], eis.at[d], eir.at[d], p, c)

    def turn(p):
        @pl.when(p == r)
        def _():
            e_rows[at_row(r), half(k)] = eall[p]

        @pl.when(p != r)
        def _():
            inplane(lax.rem(p - r + R, R) - 1, p).start()

    pair = rc(e_rows.at[:, half(k)], e_rows.at[:, half(k)], ps, pr, r, partner)

    def share(h):
        @pl.when(jnp.logical_or(z - r == h, r - z == h))
        def _():
            for d in range(R - 1):
                inplane(d, rows[d]).wait_recv()
            pair.start()

    def hop(h):
        @pl.when(z - h >= 0)
        def _():
            flow(z - h, 2).wait_recv()

            @pl.when(z < Z - 1)
            def _():
                flow(z - h, 2).start()

        @pl.when(z + h <= Z - 1)
        def _():
            flow(z + h, -2).wait_recv()

            @pl.when(z > 0)
            def _():
                flow(z + h, -2).start()

            turn(z + h)

        @pl.when(z - h >= 0)
        def _():
            turn(z - h)

        share(h - 1)

    def mucopy(d):
        return rc(mbuf.at[c], mbuf.at[c], mus.at[d], mur.at[d], r, cols[d])

    @pl.when(z < Z - 1)
    def _():
        flow(z, 2).start()

    @pl.when(z > 0)
    def _():
        flow(z, -2).start()

    turn(z)
    for d in range(N - 1):
        mucopy(d).start()

    xcopy = rc(xp.at[:, half(1 - k)], xbuf, xs, xr, r, partner)

    def mcopy(d, which):
        q = rows[d]
        return rc(acc.at[which, at_row(q)], mrecv.at[d, which], ms.at[d, which], mrs.at[d, which], q, c)

    def xcopy2(d):
        return rc(xsum.at[at_row(rows[d])], xin.at[r], xis.at[d], xir.at[d], rows[d], c)

    def upcopy(j, col):
        return rc(xin.at[j], up.at[j], ups.at[j], upr.at[j], r, col)

    def x_begin():
        @pl.when(low)
        def _():
            xcopy.start()

    def x_turn():
        @pl.when(low)
        def _():
            xcopy.wait()
            xsum[...] = xp[:, half(k)] + xbuf[...]
            xin[r] = xsum[at_row(r)]
            for d in range(R - 1):
                xcopy2(d).start()

    def climb(zz, j):
        @pl.when(z == zz)
        def _():
            @pl.when(r != j)
            def _():
                d = lax.rem(r - j + R, R)
                rc(xin.at[j], xin.at[j], xis.at[d - 1], xir.at[d - 1], j, c).wait_recv()

            if zz > 0:
                upcopy(j, c - 2).wait_recv()
                xin[j] = xin[j] + up[j]
            if zz < j:
                upcopy(j, c + 2).start()

    def e_ready():
        share(Z - 1)
        pair.wait()

        @pl.loop(0, M // 32)
        def _(i):
            rows32 = pl.ds(pl.multiple_of(i * 32, 32), 32)
            hi, lo = split(e_rows[rows32, :])
            estack[rows32, :] = hi
            estack[pl.ds(pl.multiple_of(M + i * 32, 32), 32), :] = lo

    def m_send(which):
        for d in range(R - 1):
            if which == 0:
                mcopy(d, 0).start()
            else:
                @pl.when(low)
                def _():
                    mcopy(d, 1).start()

    def x_tile(i, slot):
        where = pl.ds(x_start(i), CH)
        xp[:, where] = jnp.zeros((M, CH), F32)

        @pl.loop(0, per)
        def _(b):
            at = pl.ds(pl.multiple_of(b * CH, CH), CH)
            hi, lo = split(tiles[slot, :, at])
            both = dstack[:, at]
            dims = (((1,), (1,)), ((), ()))
            p = lax.dot_general(both, hi, dims, preferred_element_type=F32)
            q = lax.dot_general(both[:M], lo, dims, preferred_element_type=F32)
            xp[:, where] += p[:M] + p[M:] + q

    def m_tile(which, i, slot):
        @pl.loop(0, per)
        def _(b):
            at = pl.ds(pl.multiple_of(b * CH, CH), CH)
            hi, lo = split(tiles[slot, :, at])
            both = estack[:, i * CH : (i + 1) * CH]
            dims = (((1,), (0,)), ((), ()))
            p = lax.dot_general(both, hi, dims, preferred_element_type=F32)
            q = lax.dot_general(both[:M], lo, dims, preferred_element_type=F32)
            out = p[:M] + p[M:] + q
            if i == 0:
                acc[which, :, at] = out
            else:
                acc[which, :, at] += out

    @pl.loop(0, M // 32)
    def _(i):
        rows32 = pl.ds(pl.multiple_of(i * 32, 32), 32)
        old = c_prev[rows32, :]
        hi, lo = split(1.5 * old * old)
        dstack[rows32, :] = hi
        dstack[pl.ds(pl.multiple_of(M + i * 32, 32), 32), :] = lo

    hooks = {}

    def hook(n, f, *args):
        hooks.setdefault(n, []).append((f, args))

    hook(per - 1, x_begin)
    for h in range(1, Z):
        hook(min((h * count) // Z - 1 + (h > 2), count - 1), hop, h)
    hook(count - 1, e_ready)
    hook(count, x_turn)
    for zz in range(Z):
        for j in reversed(range(zz, Z)):
            hook(count + 2 + 2 * zz + (Z - 1 - j), climb, zz, j)
    hook(2 * count - 1, m_send, 0)
    hook(3 * count - 1, m_send, 1)
    for n in range(3 * count):
        if n + 2 < 3 * count:
            tile_copy(n + 2).start()
        tile_copy(n).wait()
        kind, i = divmod(n, count)
        if kind == 0:
            x_tile(i, n % SLOTS)
        else:
            m_tile(kind - 1, i, n % SLOTS)
        for f, args in hooks.get(n, ()):
            f(*args)

    for d in range(N - 1):
        mucopy(d).wait_recv()
    total = mbuf[0]
    for i in range(1, N):
        total = total + mbuf[i]
    scalar = WARMTH + coef * jnp.sum(total, axis=1, keepdims=True)
    racc[0] = acc[0, at_row(r)] + xin[z]
    racc[1] = acc[1, at_row(r)]
    for d in range(R - 1):
        mcopy(d, 0).wait_recv()
        racc[0] = racc[0] + mrecv[d, 0]
    for d in range(R - 1):
        @pl.when(z <= lax.rem(r - d - 1 + R, R))
        def _():
            mcopy(d, 1).wait_recv()
            racc[1] = racc[1] + mrecv[d, 1]

    cn = c_in[...] + STEP * (coef * racc[0] - scalar * c_in[...])
    rn = r_in[...] + STEP * (coef * racc[1] - scalar * r_in[...])
    csrc[0] = cn
    c_full[at_row(r)] = cn
    fulls = [c_full]
    if last:
        csrc[1] = rn
        r_full[at_row(r)] = rn
        fulls.append(r_full)
    else:
        c_out[...] = cn
        r_out[...] = rn

    def gcopy(d, which):
        return rc(csrc.at[which], fulls[which].at[at_row(r)], cs.at[d, which], crs.at[d, which], rows[d], c)

    for which in range(len(fulls)):
        for d in range(R - 1):
            gcopy(d, which).start()
    for d in range(N - 1):
        mucopy(d).wait_send()
    for p in range(Z):
        @pl.when(jnp.logical_and(p <= z, z < Z - 1))
        def _():
            flow(p, 2).wait_send()

        @pl.when(jnp.logical_and(p >= z, z > 0))
        def _():
            flow(p, -2).wait_send()
    for d in range(R - 1):
        inplane(d, rows[d]).wait_send()
        mcopy(d, 0).wait_send()

    @pl.when(low)
    def _():
        for d in range(R - 1):
            mcopy(d, 1).wait_send()
            xcopy2(d).wait_send()
    for j in range(Z):
        @pl.when(z < j)
        def _():
            upcopy(j, c + 2).wait_send()
    for which in range(len(fulls)):
        for d in range(R - 1):
            gcopy(d, which).wait()


def block_call(last, coef, R, Z, hc, hr, c_full, c, r):
    dma, vmem = pltpu.SemaphoreType.DMA, pltpu.VMEM
    T, U = c.shape
    M, N, CH = R * T, 2 * Z, U // 4
    scratch = [
        vmem((SLOTS, CH, U), F32),
        vmem((M, 2 * U), F32),
        vmem((2, M, U), F32),
        vmem((M, 2 * U), F32),
        vmem((2 * M, 2 * U), BF16),
        vmem((2 * M, U), BF16),
        vmem((M, U), F32),
        vmem((M, U), F32),
        vmem((R, T, U), F32),
        vmem((Z, T, U), F32),
        vmem((R - 1, 2, T, U), F32),
        vmem((2, T, U), F32),
        vmem((2, T, U), F32),
        vmem((Z, T, U), F32),
        vmem((N, T, 128), F32),
        dma((SLOTS,)),
    ]
    scratch += [dma, dma, dma((R - 1,)), dma((R - 1,)), dma((Z,)), dma((Z,))] + [dma((R - 1, 2))] * 4
    scratch += [dma((Z,))] * 4 + [dma((R - 1,))] * 2 + [dma, dma] + [dma((N - 1,))] * 2
    piece, full = (T, U), (M, U)
    shapes = (full, full) if last else (piece, piece, full)
    spec, hbm = pl.BlockSpec(memory_space=pltpu.VMEM), pl.BlockSpec(memory_space=pl.ANY)
    return pl.pallas_call(
        functools.partial(block_kernel, last, coef, R, Z),
        out_shape=[jax.ShapeDtypeStruct(s, F32) for s in shapes],
        in_specs=[hbm, hbm, spec, spec, spec],
        out_specs=[spec] * len(shapes),
        scratch_shapes=scratch,
        name="block_last" if last else "block_mid",
        compiler_params=pltpu.CompilerParams(collective_id=2 if last else 1, has_side_effects=True),
    )(hc, hr, c_full, c, r)


def kernel_body(hist_corr, hist_resp, row_corr, row_resp):
    R, N = lax.axis_size("row"), lax.axis_size("col")
    T = row_corr.shape[0] // R
    coef = 1.0 / math.sqrt(hist_corr.shape[0] * R)
    start = lax.axis_index("row") * T
    corr = lax.dynamic_slice_in_dim(row_corr, start, T, 0)
    resp = lax.dynamic_slice_in_dim(row_resp, start, T, 0)
    full = row_corr
    for _ in range(BLOCKS - 1):
        corr, resp, full = block_call(False, coef, R, N // 2, hist_corr, hist_resp, full, corr, resp)
    return tuple(block_call(True, coef, R, N // 2, hist_corr, hist_resp, full, corr, resp))


def solution(mesh):
    R, N = mesh.shape["row"], mesh.shape["col"]
    body = kernel_body if N == 2 * R and R == 4 else plain_body
    in_specs = (P("row", "col"), P("row", "col"), P(None, "col"), P(None, "col"))
    out_specs = (P(None, "col"), P(None, "col"))
    return jax.shard_map(body, mesh=mesh, in_specs=in_specs, out_specs=out_specs, check_vma=False)
```

time: 1190 us -> 483 us (0.41)
  Pallas kernels: 0 us -> 467 us
  waiting for transfers between devices: 392 us -> 0 us
  blocking collectives: 333 us -> 0 us
  matrix products: 330 us -> 0 us
  starting transfers between devices: 51.2 us -> 0 us
  local copies, waits for them, and re-layouts: 43.7 us -> 6.45 us
  between operations: 16.3 us -> 0.67 us
  other arithmetic: 14.3 us -> 0 us
    pallas_call x0 -> x4, Pallas kernels: none -> 467 us  [block_call(): pl.pallas_call(functools.partial(block_kernel, last, coef, R, Z), out_sha...]
    psum x8 -> x0, waiting for transfers between devices: 392 us -> none  [the longest x4 258 us: body(): cross_total = lax.psum(part_cross, 'col')]
    dot_general x12 -> x0, matrix products: 330 us -> none  [the longest x4 151 us: body(): lax.dot_general(slope_contribution, hist_resp, (((1,), (1,)), ((), ())),...]
    all_to_all x4 -> x0, blocking collectives: 216 us -> none  [turn_rows(): lax.all_to_all(spread, 'col', split_axis=0, concat_axis=1, tiled=True)]
    psum x4 -> x0, blocking collectives: 117 us -> none  [body(): enforcing_scalar_sum = lax.psum(multiplier_terms, 'col')]
    all_to_all x12 -> x0, starting transfers between devices: 49 us -> none  [the longest x4 18 us: turn_rows(): lax.all_to_all(lax.all_to_all(spread, 'col', split_axis=0, concat_axis=1,...]
    reshape x8 -> x0, local copies, waits for them, and re-layouts: 17 us -> none  [the longest x4 12.6 us: turn_cols(): blocks = values.reshape(values.shape[0], factor, block_span)]
  transfers between devices with their start and end apart: 20 -> 0, of which waited for: 8 -> 0; matrix products, arithmetic and copies ran while one was open for 31% -> 0% of each run, Pallas kernels for 0% -> 0%
where the time goes in v1:
time: 483 us; the launch traced here: 474 us
  Pallas kernels  467 us (97%)
  local copies, waits for them, and re-layouts  6.45 us (1%)
    pallas_call x4, Pallas kernels, block_call(): pl.pallas_call(functools.partial(block_kernel, last, coef, R, Z), out_sha...  467 us

profile of v1, /device:TPU:0, one launch (start us, length us, event | category | flops | bytes accessed | tf_op | source)
XLA Modules:
  0.0 473.8 jit_solution(9966456010261852153)
XLA Ops:
  0.6 1.9 constant_dynamic-slice_fusion
  2.5 108.8 %block_mid.3 = (f32[32,2048]{1,0:T(8,128)}, f32[32,2048]{1,0:T(8,128)}, f32[128,2048]{1,0:T(8,128)}) custom-call(f32[4096,2048]{1,0:T(8,128)} %hc.7, f32[4096,2048]{1,0:T(8,128)} %hr.7, f32[128,2048]{1,0:T(8,128)} %c_prev.1, f32[32,2048]{1,0:T(8,128)} %get-tuple-element.21.c_in, f32[32,2048]{1,0:T(8,128)} %get-tuple-element.20.r_in), custom_call_target="tpu_custom_call" | custom-call | tf_op jit(solution)/shard_map/block_mid/pallas_call | solution.py:412
  111.3 115.4 %block_mid.4 = (f32[32,2048]{1,0:T(8,128)}, f32[32,2048]{1,0:T(8,128)}, f32[128,2048]{1,0:T(8,128)}) custom-call(f32[4096,2048]{1,0:T(8,128)} %hc.7, f32[4096,2048]{1,0:T(8,128)} %hr.7, f32[128,2048]{1,0:T(8,128)} %get-tuple-element.11.c_prev, f32[32,2048]{1,0:T(8,128)} %get-tuple-element.12.c_in, f32[32,2048]{1,0:T(8,128)} %get-tuple-element.13.r_in), custom_call_target="tpu_custom_call" | custom-call | tf_op jit(solution)/shard_map/block_mid/pallas_call | solution.py:412
  226.7 115.7 %block_mid.5 = (f32[32,2048]{1,0:T(8,128)}, f32[32,2048]{1,0:T(8,128)}, f32[128,2048]{1,0:T(8,128)}) custom-call(f32[4096,2048]{1,0:T(8,128)} %hc.7, f32[4096,2048]{1,0:T(8,128)} %hr.7, f32[128,2048]{1,0:T(8,128)} %get-tuple-element.14.c_prev, f32[32,2048]{1,0:T(8,128)} %get-tuple-element.15.c_in, f32[32,2048]{1,0:T(8,128)} %get-tuple-element.16.r_in), custom_call_target="tpu_custom_call" | custom-call | tf_op jit(solution)/shard_map/block_mid/pallas_call | solution.py:412
  342.4 126.8 %block_last.1 = (f32[128,2048]{1,0:T(8,128)}, f32[128,2048]{1,0:T(8,128)}) custom-call(f32[4096,2048]{1,0:T(8,128)} %hc.7, f32[4096,2048]{1,0:T(8,128)} %hr.7, f32[128,2048]{1,0:T(8,128)} %get-tuple-element.17.c_prev, f32[32,2048]{1,0:T(8,128)} %get-tuple-element.18.c_in, f32[32,2048]{1,0:T(8,128)} %get-tuple-element.19.r_in), custom_call_target="tpu_custom_call" | custom-call | tf_op jit(solution)/shard_map/block_last/pallas_call | solution.py:412
  469.2 2.3 copy.8
  471.5 2.3 copy.9
